TPU v7x, 32 devices: a whole 2x2x4 slice. The times are simulated.
32 devices in a mesh: segment: 4 (over y, x), dom: 8 (over z, core).
Axes of the slice: x: 2, y: 2, z: 4, core: 2. Of those that a mesh axis runs over, the one named last changes fastest.
Arguments:
- samples: bfloat16 [4, 4096, 512], P(None, 'dom'), may hold values from -6 to 6
- w_source: bfloat16 [4, 1, 512, 512], P('segment'), may hold values from -0.25 to 0.25
- w_self: bfloat16 [4, 1, 512, 512], P('segment'), may hold values from -0.25 to 0.25
- w_message: bfloat16 [4, 1, 512, 512], P('segment'), may hold values from -0.25 to 0.25
- w_output: bfloat16 [4, 1, 512, 512], P('segment'), may hold values from -0.25 to 0.25
- norm_gain: float32 [4, 1, 512], P('segment'), may hold values from 0.1 to 1.9
- tile_source: int32 [4, 32, 6], P('segment', 'dom'), may hold values from 0 to 31, as said below
- tile_count: int32 [4, 32], P('segment', 'dom'), may hold values from 3 to 6, as said below
- tile_value: bfloat16 [4, 32, 6, 128, 128], P('segment', 'dom'), may hold values from -0.21875 to 0.21875
Outputs:
- final: bfloat16 [4, 4096, 512], P('segment', 'dom')
Inputs may be any that keep to these rules, and one draw needn't show every extreme that they name: `tile_source`: each entry for destination block b names a block among the 4 blocks that hold b's dom index (blocks (b // 4) * 4 .. + 4 - 1) or the 1 block on either side of them, counted cyclically over 32. `tile_count`: slots at or beyond the count are unused; the first block of every dom index uses all 6 slots.
All inputs are finite; a program needn't handle non-finite values.
Results may differ from a plain program's by a relative error of at most 0.013.
Values may be sent and summed in bfloat16 or wider, within the bound.
A program may use at most 64 MiB of HBM per device.

v0:
```python
import jax
import jax.numpy as jnp
from jax import lax
from jax.sharding import PartitionSpec as P

HB = 1


def extended(cells, sides, width):
    for axis, dim in sides:
        count = lax.axis_size(axis)
        head = lax.slice_in_dim(cells, 0, width, axis=dim)
        tail = lax.slice_in_dim(cells, cells.shape[dim] - width, cells.shape[dim], axis=dim)
        cells = jnp.concatenate(
            [
                lax.ppermute(tail, axis, [(i, (i + 1) % count) for i in range(count)]),
                cells,
                lax.ppermute(head, axis, [((i + 1) % count, i) for i in range(count)]),
            ],
            axis=dim,
        )
    return cells


def from_behind(shard, axis, by):
    count = lax.axis_size(axis)
    pairs = [(i, i + by) for i in range(count) if 0 <= i + by < count]
    return lax.ppermute(shard, axis, pairs)


def run_layer(h, w_source, w_self, w_message, w_output, norm_gain, sources, counts, tiles):
    blocks = sources.shape[0]
    block_rows = tiles.shape[-1]
    width = h.shape[1]
    dom_index = lax.axis_index("dom")
    total_blocks = blocks * lax.axis_size("dom")
    sender = jax.nn.silu(jnp.dot(h, w_source, preferred_element_type=jnp.float32)).astype(
        jnp.bfloat16
    )
    reach = HB
    padded = extended(sender, (("dom", 0),), HB * block_rows)
    first_block = dom_index * blocks - reach
    local_index = jnp.mod(sources - first_block, total_blocks)
    padded_blocks = padded.reshape(padded.shape[0] // block_rows, block_rows, width)
    picked = padded_blocks[local_index]
    keep = (jnp.arange(sources.shape[1], dtype=jnp.int32)[None, :] < counts[:, None]).astype(
        jnp.bfloat16
    )
    weights = tiles * keep[:, :, None, None]
    gathered = jnp.einsum("bkij,bkjd->bid", weights, picked, preferred_element_type=jnp.float32)
    gathered = gathered.reshape(blocks * block_rows, width).astype(jnp.bfloat16)
    mixed = jnp.dot(h, w_self, preferred_element_type=jnp.float32) + jnp.dot(
        gathered, w_message, preferred_element_type=jnp.float32
    )
    scaled = mixed / jnp.sqrt(jnp.mean(mixed * mixed, axis=-1, keepdims=True) + 1e-05) * norm_gain
    update = jax.nn.silu(scaled).astype(jnp.bfloat16)
    return (
        h.astype(jnp.float32) + jnp.dot(update, w_output, preferred_element_type=jnp.float32)
    ).astype(jnp.bfloat16)


def shards(
    samples, w_source, w_self, w_message, w_output, norm_gain, tile_source, tile_count, tile_value
):
    sections = lax.axis_size("segment")
    segment_index = lax.axis_index("segment")
    sample_total = samples.shape[0]
    incoming = samples[0]
    finished = []
    for step in range(sample_total + sections - 1):
        entering = samples[min(step, sample_total - 1)]
        h = jnp.where(segment_index == 0, entering, incoming)
        h = run_layer(
            h,
            w_source[0, 0],
            w_self[0, 0],
            w_message[0, 0],
            w_output[0, 0],
            norm_gain[0, 0],
            tile_source[0],
            tile_count[0],
            tile_value[0],
        )
        if step >= sections - 1:
            finished.append(h)
        incoming = from_behind(h, "segment", 1)
    stacked = jnp.stack(finished)
    kept = jnp.where(segment_index == sections - 1, stacked, jnp.zeros_like(stacked))
    moved = lax.all_to_all(kept, "segment", split_axis=0, concat_axis=0, tiled=True)
    moved = moved.reshape(sections, sample_total // sections, moved.shape[1], moved.shape[2])
    return jnp.sum(moved.astype(jnp.float32), axis=0).astype(jnp.bfloat16)


def solution(mesh):
    return jax.shard_map(
        shards,
        mesh=mesh,
        in_specs=(
            P(None, "dom", None),
            P("segment", None, None, None),
            P("segment", None, None, None),
            P("segment", None, None, None),
            P("segment", None, None, None),
            P("segment", None, None),
            P("segment", "dom", None),
            P("segment", "dom"),
            P("segment", "dom", None, None, None),
        ),
        out_specs=P("segment", "dom", None),
        check_vma=False,
    )
```

profile of v0, /device:TPU:4, one launch (start us, length us, event | category | flops | bytes accessed | tf_op | source)
XLA Modules:
  0.0 240.6 jit_solution(7820811586883428880)
XLA Ops:
  0.0 1.9 multiply_convert_fusion.13
  2.0 3.5 %collective-permute-start.1 = (bf16[128,512]{0,1:T(8,128)(2,1)S(1)}, bf16[128,512]{0,1:T(8,128)(2,1)S(1)}, u32[]{:S(2)}, u32[]{:S(2)}) collective-permute-start(bf16[128,512]{0,1:T(8,128)(2,1)S(1)} %get-tuple-element.18), channel_id=1, source_target_pairs={{1,0},{2,1},{3,2},{4,3},{5,4},{6,5},{7,6},{0,7},{9,8},{10,9},{11,1... | collective-permute-start | bytes 393224 | tf_op jit(solution)/shard_map/ppermute | solution.py:18
  5.5 2.5 %fusion.81 = f32[512,512]{0,1:T(8,128)} fusion(bf16[1,1,512,512]{3,2,1,0:T(8,128)(2,1)S(1)} %copy-done, bf16[4,512,512]{2,1,0:T(8,128)(2,1)} %param.9), kind=kOutput, calls=%fused_computation.113 | convolution fusion | flops 268435456 | bytes 2097152 | tf_op jit(solution)/shard_map/dot_general | solution.py:52
  8.7 2.5 %gather_fusion = bf16[24,128,512]{2,1,0:T(8,128)(2,1)} fusion(bf16[6,128,512]{2,1,0:T(8,128)(2,1)S(1)} %bitcast.221, s32[1024]{0:T(1024)S(1)} %pad_clamp_fusion), kind=kCustom, calls=%fused_computation | custom fusion | bytes 6291552 | tf_op jit(solution)/shard_map/gather | solution.py:45
  11.2 2.6 %fusion = bf16[4,128,512]{2,1,0:T(8,128)(2,1)S(1)} fusion(bf16[4,6,128,512]{3,2,1,0:T(8,128)(2,1)} %bitcast.228, bf16[1,4,6,128,128]{4,3,2,1,0:T(8,128)(2,1)S(1)} %copy-done.1, bf16[4,6]{1,0:T(4,128)(2,1)S(1)} %fusion.103), kind=kOutput, calls=%fused_computation.23 | convolution fusion | flops 403308544 | bytes 4456496 | tf_op jit(solution)/shard_map/bkij,bkjd->bid/dot_general | solution.py:50
  14.9 2.7 %fusion.7 = bf16[512,512]{1,0:T(8,128)(2,1)} fusion(f32[512,512]{0,1:T(8,128)S(1)} %get-tuple-element.20, bf16[1,1,512,512]{3,2,1,0:T(8,128)(2,1)S(1)} %copy-done.29, f32[512]{0:T(512)S(1)} %bitcast.244, f32[512]{0:T(512)S(1)} %add_sqrt_fusion.6, bf16[4,512,512]{2,1,0:T(8,128)(2,1)} %param.9), kind=kOutput, calls=%fused_computation.30 | convolution fusion | flops 271056896 | bytes 2625536 | tf_op jit(solution)/shard_map/dot_general | solution.py:58
  17.6 3.4 %collective-permute-start.2 = (bf16[512,512]{1,0:T(8,128)(2,1)}, bf16[512,512]{1,0:T(8,128)(2,1)S(1)}, u32[]{:S(2)}, u32[]{:S(2)}) collective-permute-start(bf16[512,512]{1,0:T(8,128)(2,1)} %fusion.7), channel_id=1, source_target_pairs={{0,8},{8,16},{16,24},{1,9},{9,17},{17,25},{2,10},{10,18},{18,26},{... | collective-permute-start | bytes 1572872 | tf_op jit(solution)/shard_map/ppermute | solution.py:28
  21.0 14.2 %collective-permute-done.2 = bf16[512,512]{1,0:T(8,128)(2,1)S(1)} collective-permute-done((bf16[512,512]{1,0:T(8,128)(2,1)}, bf16[512,512]{1,0:T(8,128)(2,1)S(1)}, u32[]{:S(2)}, u32[]{:S(2)}) %collective-permute-start.2) | collective-permute-done | bytes 524320 | tf_op jit(solution)/shard_map/ppermute | solution.py:28
  35.2 1.1 bitcast_select_fusion
  37.3 3.4 %collective-permute-start.4 = (bf16[128,512]{0,1:T(8,128)(2,1)S(1)}, bf16[128,512]{0,1:T(8,128)(2,1)S(1)}, u32[]{:S(2)}, u32[]{:S(2)}) collective-permute-start(bf16[128,512]{0,1:T(8,128)(2,1)S(1)} %get-tuple-element.16), channel_id=1, source_target_pairs={{1,0},{2,1},{3,2},{4,3},{5,4},{6,5},{7,6},{0,7},{9,8},{10,9},{11,1... | collective-permute-start | bytes 393224 | tf_op jit(solution)/shard_map/ppermute | solution.py:18
  40.7 3.4 %collective-permute-done.3 = bf16[128,512]{0,1:T(8,128)(2,1)S(1)} collective-permute-done((bf16[128,512]{0,1:T(8,128)(2,1)S(1)}, bf16[128,512]{0,1:T(8,128)(2,1)S(1)}, u32[]{:S(2)}, u32[]{:S(2)}) %collective-permute-start.3) | collective-permute-done | bytes 131104 | tf_op jit(solution)/shard_map/ppermute | solution.py:16
  44.5 2.5 %gather_fusion.1 = bf16[24,128,512]{2,1,0:T(8,128)(2,1)} fusion(bf16[6,128,512]{2,1,0:T(8,128)(2,1)S(1)} %bitcast.222, s32[1024]{0:T(1024)S(1)} %pad_clamp_fusion), kind=kCustom, calls=%fused_computation.1 | custom fusion | bytes 6291552 | tf_op jit(solution)/shard_map/gather | solution.py:45
  47.0 2.5 %fusion.1 = bf16[4,128,512]{2,1,0:T(8,128)(2,1)S(1)} fusion(bf16[4,6,128,512]{3,2,1,0:T(8,128)(2,1)} %bitcast.229, bf16[1,4,6,128,128]{4,3,2,1,0:T(8,128)(2,1)S(1)} %copy-done.1, bf16[4,6]{1,0:T(4,128)(2,1)S(1)} %fusion.103), kind=kOutput, calls=%fused_computation.24 | convolution fusion | flops 403308544 | bytes 4456496 | tf_op jit(solution)/shard_map/bkij,bkjd->bid/dot_general | solution.py:50
  52.4 2.5 %collective-permute-start.5 = (bf16[512,512]{1,0:T(8,128)(2,1)S(1)}, bf16[512,512]{1,0:T(8,128)(2,1)S(1)}, u32[]{:S(2)}, u32[]{:S(2)}) collective-permute-start(bf16[512,512]{1,0:T(8,128)(2,1)S(1)} %add_convert_fusion.5), channel_id=1, source_target_pairs={{0,8},{8,16},{16,24},{1,9},{9,17},{17,25},{2,10},{10,18},{18,26},{... | collective-permute-start | bytes 1572872 | tf_op jit(solution)/shard_map/ppermute | solution.py:28
  54.9 13.6 %collective-permute-done.5 = bf16[512,512]{1,0:T(8,128)(2,1)S(1)} collective-permute-done((bf16[512,512]{1,0:T(8,128)(2,1)S(1)}, bf16[512,512]{1,0:T(8,128)(2,1)S(1)}, u32[]{:S(2)}, u32[]{:S(2)}) %collective-permute-start.5) | collective-permute-done | bytes 524320 | tf_op jit(solution)/shard_map/ppermute | solution.py:28
  68.5 1.1 bitcast_select_fusion.1
  70.5 3.5 %collective-permute-start.7 = (bf16[128,512]{0,1:T(8,128)(2,1)S(1)}, bf16[128,512]{0,1:T(8,128)(2,1)S(1)}, u32[]{:S(2)}, u32[]{:S(2)}) collective-permute-start(bf16[128,512]{0,1:T(8,128)(2,1)S(1)} %get-tuple-element.14), channel_id=1, source_target_pairs={{1,0},{2,1},{3,2},{4,3},{5,4},{6,5},{7,6},{0,7},{9,8},{10,9},{11,1... | collective-permute-start | bytes 393224 | tf_op jit(solution)/shard_map/ppermute | solution.py:18
  74.0 2.6 %collective-permute-done.6 = bf16[128,512]{0,1:T(8,128)(2,1)S(1)} collective-permute-done((bf16[128,512]{0,1:T(8,128)(2,1)S(1)}, bf16[128,512]{0,1:T(8,128)(2,1)S(1)}, u32[]{:S(2)}, u32[]{:S(2)}) %collective-permute-start.6) | collective-permute-done | bytes 131104 | tf_op jit(solution)/shard_map/ppermute | solution.py:16
  77.0 2.5 %gather_fusion.2 = bf16[24,128,512]{2,1,0:T(8,128)(2,1)} fusion(bf16[6,128,512]{2,1,0:T(8,128)(2,1)S(1)} %bitcast.223, s32[1024]{0:T(1024)S(1)} %pad_clamp_fusion), kind=kCustom, calls=%fused_computation.2 | custom fusion | bytes 6291552 | tf_op jit(solution)/shard_map/gather | solution.py:45
  79.5 2.5 %fusion.2 = bf16[4,128,512]{2,1,0:T(8,128)(2,1)S(1)} fusion(bf16[4,6,128,512]{3,2,1,0:T(8,128)(2,1)} %bitcast.230, bf16[1,4,6,128,128]{4,3,2,1,0:T(8,128)(2,1)S(1)} %copy-done.1, bf16[4,6]{1,0:T(4,128)(2,1)S(1)} %fusion.103), kind=kOutput, calls=%fused_computation.25 | convolution fusion | flops 403308544 | bytes 4456496 | tf_op jit(solution)/shard_map/bkij,bkjd->bid/dot_general | solution.py:50
  84.9 2.3 collective-permute-start.8
  87.2 12.1 %collective-permute-done.8 = bf16[512,512]{1,0:T(8,128)(2,1)S(1)} collective-permute-done((bf16[512,512]{1,0:T(8,128)(2,1)S(1)}, bf16[512,512]{1,0:T(8,128)(2,1)S(1)}, u32[]{:S(2)}, u32[]{:S(2)}) %collective-permute-start.8) | collective-permute-done | bytes 524320 | tf_op jit(solution)/shard_map/ppermute | solution.py:28
  99.3 1.1 bitcast_select_fusion.5
  101.3 3.5 %collective-permute-start.10 = (bf16[128,512]{0,1:T(8,128)(2,1)S(1)}, bf16[128,512]{0,1:T(8,128)(2,1)S(1)}, u32[]{:S(2)}, u32[]{:S(2)}) collective-permute-start(bf16[128,512]{0,1:T(8,128)(2,1)S(1)} %get-tuple-element.12), channel_id=1, source_target_pairs={{1,0},{2,1},{3,2},{4,3},{5,4},{6,5},{7,6},{0,7},{9,8},{10,9},{11,1... | collective-permute-start | bytes 393224 | tf_op jit(solution)/shard_map/ppermute | solution.py:18
  104.8 2.6 %collective-permute-done.9 = bf16[128,512]{0,1:T(8,128)(2,1)S(1)} collective-permute-done((bf16[128,512]{0,1:T(8,128)(2,1)S(1)}, bf16[128,512]{0,1:T(8,128)(2,1)S(1)}, u32[]{:S(2)}, u32[]{:S(2)}) %collective-permute-start.9) | collective-permute-done | bytes 131104 | tf_op jit(solution)/shard_map/ppermute | solution.py:16
  107.8 2.5 %gather_fusion.3 = bf16[24,128,512]{2,1,0:T(8,128)(2,1)} fusion(bf16[6,128,512]{2,1,0:T(8,128)(2,1)S(1)} %bitcast.224, s32[1024]{0:T(1024)S(1)} %pad_clamp_fusion), kind=kCustom, calls=%fused_computation.3 | custom fusion | bytes 6291552 | tf_op jit(solution)/shard_map/gather | solution.py:45
  110.3 2.5 %fusion.3 = bf16[4,128,512]{2,1,0:T(8,128)(2,1)S(1)} fusion(bf16[4,6,128,512]{3,2,1,0:T(8,128)(2,1)} %bitcast.231, bf16[1,4,6,128,128]{4,3,2,1,0:T(8,128)(2,1)S(1)} %copy-done.1, bf16[4,6]{1,0:T(4,128)(2,1)S(1)} %fusion.103), kind=kOutput, calls=%fused_computation.26 | convolution fusion | flops 403308544 | bytes 4456496 | tf_op jit(solution)/shard_map/bkij,bkjd->bid/dot_general | solution.py:50
  115.8 1.9 collective-permute-start.11
  117.7 13.0 %collective-permute-done.11 = bf16[512,512]{1,0:T(8,128)(2,1)S(1)} collective-permute-done((bf16[512,512]{1,0:T(8,128)(2,1)S(1)}, bf16[512,512]{1,0:T(8,128)(2,1)S(1)}, u32[]{:S(2)}, u32[]{:S(2)}) %collective-permute-start.11) | collective-permute-done | bytes 524320 | tf_op jit(solution)/shard_map/ppermute | solution.py:28
  130.7 1.1 bitcast_select_fusion.4
  132.7 3.5 %collective-permute-start.13 = (bf16[128,512]{0,1:T(8,128)(2,1)S(1)}, bf16[128,512]{0,1:T(8,128)(2,1)S(1)}, u32[]{:S(2)}, u32[]{:S(2)}) collective-permute-start(bf16[128,512]{0,1:T(8,128)(2,1)S(1)} %get-tuple-element.10), channel_id=1, source_target_pairs={{1,0},{2,1},{3,2},{4,3},{5,4},{6,5},{7,6},{0,7},{9,8},{10,9},{11,1... | collective-permute-start | bytes 393224 | tf_op jit(solution)/shard_map/ppermute | solution.py:18
  136.2 2.7 %collective-permute-done.12 = bf16[128,512]{0,1:T(8,128)(2,1)S(1)} collective-permute-done((bf16[128,512]{0,1:T(8,128)(2,1)S(1)}, bf16[128,512]{0,1:T(8,128)(2,1)S(1)}, u32[]{:S(2)}, u32[]{:S(2)}) %collective-permute-start.12) | collective-permute-done | bytes 131104 | tf_op jit(solution)/shard_map/ppermute | solution.py:16
  139.3 2.5 %gather_fusion.4 = bf16[24,128,512]{2,1,0:T(8,128)(2,1)} fusion(bf16[6,128,512]{2,1,0:T(8,128)(2,1)S(1)} %bitcast.225, s32[1024]{0:T(1024)S(1)} %pad_clamp_fusion), kind=kCustom, calls=%fused_computation.4 | custom fusion | bytes 6291552 | tf_op jit(solution)/shard_map/gather | solution.py:45
  141.8 2.5 %fusion.4 = bf16[4,128,512]{2,1,0:T(8,128)(2,1)S(1)} fusion(bf16[4,6,128,512]{3,2,1,0:T(8,128)(2,1)} %bitcast.232, bf16[1,4,6,128,128]{4,3,2,1,0:T(8,128)(2,1)S(1)} %copy-done.1, bf16[4,6]{1,0:T(4,128)(2,1)S(1)} %fusion.103), kind=kOutput, calls=%fused_computation.27 | convolution fusion | flops 403308544 | bytes 4456496 | tf_op jit(solution)/shard_map/bkij,bkjd->bid/dot_general | solution.py:50
  147.3 1.9 collective-permute-start.14
  149.2 14.7 %collective-permute-done.14 = bf16[512,512]{1,0:T(8,128)(2,1)S(1)} collective-permute-done((bf16[512,512]{1,0:T(8,128)(2,1)S(1)}, bf16[512,512]{1,0:T(8,128)(2,1)S(1)}, u32[]{:S(2)}, u32[]{:S(2)}) %collective-permute-start.14) | collective-permute-done | bytes 524320 | tf_op jit(solution)/shard_map/ppermute | solution.py:28
  165.9 3.5 %collective-permute-start.16 = (bf16[128,512]{0,1:T(8,128)(2,1)S(1)}, bf16[128,512]{0,1:T(8,128)(2,1)S(1)}, u32[]{:S(2)}, u32[]{:S(2)}) collective-permute-start(bf16[128,512]{0,1:T(8,128)(2,1)S(1)} %get-tuple-element.8), channel_id=1, source_target_pairs={{1,0},{2,1},{3,2},{4,3},{5,4},{6,5},{7,6},{0,7},{9,8},{10,9},{11,1... | collective-permute-start | bytes 393224 | tf_op jit(solution)/shard_map/ppermute | solution.py:18
  169.5 2.6 %collective-permute-done.15 = bf16[128,512]{0,1:T(8,128)(2,1)S(1)} collective-permute-done((bf16[128,512]{0,1:T(8,128)(2,1)S(1)}, bf16[128,512]{0,1:T(8,128)(2,1)S(1)}, u32[]{:S(2)}, u32[]{:S(2)}) %collective-permute-start.15) | collective-permute-done | bytes 131104 | tf_op jit(solution)/shard_map/ppermute | solution.py:16
  172.5 2.5 %gather_fusion.5 = bf16[24,128,512]{2,1,0:T(8,128)(2,1)} fusion(bf16[6,128,512]{2,1,0:T(8,128)(2,1)S(1)} %bitcast.226, s32[1024]{0:T(1024)S(1)} %pad_clamp_fusion), kind=kCustom, calls=%fused_computation.5 | custom fusion | bytes 6291552 | tf_op jit(solution)/shard_map/gather | solution.py:45
  175.0 2.5 %fusion.5 = bf16[4,128,512]{2,1,0:T(8,128)(2,1)S(1)} fusion(bf16[4,6,128,512]{3,2,1,0:T(8,128)(2,1)} %bitcast.233, bf16[1,4,6,128,128]{4,3,2,1,0:T(8,128)(2,1)S(1)} %copy-done.1, bf16[4,6]{1,0:T(4,128)(2,1)S(1)} %fusion.103), kind=kOutput, calls=%fused_computation.28 | convolution fusion | flops 403308544 | bytes 4456496 | tf_op jit(solution)/shard_map/bkij,bkjd->bid/dot_general | solution.py:50
  180.4 1.9 collective-permute-start.17
  182.3 12.1 %collective-permute-done.17 = bf16[512,512]{1,0:T(8,128)(2,1)S(1)} collective-permute-done((bf16[512,512]{1,0:T(8,128)(2,1)S(1)}, bf16[512,512]{1,0:T(8,128)(2,1)S(1)}, u32[]{:S(2)}, u32[]{:S(2)}) %collective-permute-start.17) | collective-permute-done | bytes 524320 | tf_op jit(solution)/shard_map/ppermute | solution.py:28
  196.5 3.5 %collective-permute-start.19 = (bf16[128,512]{0,1:T(8,128)(2,1)S(1)}, bf16[128,512]{0,1:T(8,128)(2,1)S(1)}, u32[]{:S(2)}, u32[]{:S(2)}) collective-permute-start(bf16[128,512]{0,1:T(8,128)(2,1)S(1)} %get-tuple-element.6), channel_id=1, source_target_pairs={{1,0},{2,1},{3,2},{4,3},{5,4},{6,5},{7,6},{0,7},{9,8},{10,9},{11,1... | collective-permute-start | bytes 393224 | tf_op jit(solution)/shard_map/ppermute | solution.py:18
  200.0 2.7 %collective-permute-done.18 = bf16[128,512]{0,1:T(8,128)(2,1)S(1)} collective-permute-done((bf16[128,512]{0,1:T(8,128)(2,1)S(1)}, bf16[128,512]{0,1:T(8,128)(2,1)S(1)}, u32[]{:S(2)}, u32[]{:S(2)}) %collective-permute-start.18) | collective-permute-done | bytes 131104 | tf_op jit(solution)/shard_map/ppermute | solution.py:16
  203.1 2.5 %gather_fusion.6 = bf16[24,128,512]{2,1,0:T(8,128)(2,1)} fusion(bf16[6,128,512]{2,1,0:T(8,128)(2,1)S(1)} %bitcast.220, s32[1024]{0:T(1024)S(1)} %pad_clamp_fusion), kind=kCustom, calls=%fused_computation.6 | custom fusion | bytes 6291552 | tf_op jit(solution)/shard_map/gather | solution.py:45
  205.6 2.5 %fusion.6 = bf16[4,128,512]{2,1,0:T(8,128)(2,1)S(1)} fusion(bf16[4,6,128,512]{3,2,1,0:T(8,128)(2,1)} %bitcast.227, bf16[1,4,6,128,128]{4,3,2,1,0:T(8,128)(2,1)S(1)} %copy-done.1, bf16[4,6]{1,0:T(4,128)(2,1)S(1)} %fusion.103), kind=kOutput, calls=%fused_computation.29 | convolution fusion | flops 403308544 | bytes 4456496 | tf_op jit(solution)/shard_map/bkij,bkjd->bid/dot_general | solution.py:50
  211.8 25.9 %all_to_all.5 = bf16[4,512,512]{2,1,0:T(8,128)(2,1)} all-to-all(bf16[4,512,512]{2,1,0:T(8,128)(2,1)S(1)} %maximum_select_fusion), channel_id=1, replica_groups=mesh['segment'=4,'dom'=8] {'segment'}, dimensions={0} | all-to-all | bytes 4194304 | tf_op jit(solution)/shard_map/all_to_all | solution.py:89
  237.7 2.9 %reduce_sum.84 = bf16[512,512]{1,0:T(8,128)(2,1)} reduce(bf16[4,512,512]{2,1,0:T(8,128)(2,1)} %all_to_all.5, bf16[]{:T(256)} %constant.83.clone.1), dimensions={0}, to_apply=%region_7.8 | reduce | flops 786432 | bytes 2621442 | tf_op jit(solution)/shard_map/reduce_sum | solution.py:91
  (151 shorter events, 29.4 us)
Async XLA Ops:
  0.0 5.5 %copy-start = (bf16[1,1,512,512]{3,2,1,0:T(8,128)(2,1)S(1)}, bf16[1,1,512,512]{3,2,1,0:T(8,128)(2,1)}, u32[]{:S(2)}) copy-start(bf16[1,1,512,512]{3,2,1,0:T(8,128)(2,1)} %param.11) | copy-start | bytes 1572868
  1.9 6.2 %copy-start.22 = (s32[1,4,6]{2,1,0:T(4,128)S(1)}, s32[1,4,6]{2,1,0:T(4,128)}, u32[]{:S(2)}) copy-start(s32[1,4,6]{2,1,0:T(4,128)} %param.15) | copy-start | bytes 292
  1.9 6.2 %copy-start.37 = (s32[1,4]{1,0:T(1,128)S(1)}, s32[1,4]{1,0:T(1,128)}, u32[]{:S(2)}) copy-start(s32[1,4]{1,0:T(1,128)} %param.16) | copy-start | bytes 52
  2.0 6.3 %collective-permute-start = (bf16[128,512]{0,1:T(8,128)(2,1)S(1)}, bf16[128,512]{0,1:T(8,128)(2,1)S(1)}, u32[]{:S(2)}, u32[]{:S(2)}) collective-permute-start(bf16[128,512]{0,1:T(8,128)(2,1)S(1)} %get-tuple-element.17), channel_id=1, source_target_pairs={{0,1},{1,2},{2,3},{3,4},{4,5},{5,6},{6,7},{7,0},{8,9},{9,10},{10,1... | collective-permute-start | bytes 393224 | tf_op jit(solution)/shard_map/ppermute | solution.py:16
  2.0 6.3 %collective-permute-start.1 = (bf16[128,512]{0,1:T(8,128)(2,1)S(1)}, bf16[128,512]{0,1:T(8,128)(2,1)S(1)}, u32[]{:S(2)}, u32[]{:S(2)}) collective-permute-start(bf16[128,512]{0,1:T(8,128)(2,1)S(1)} %get-tuple-element.18), channel_id=1, source_target_pairs={{1,0},{2,1},{3,2},{4,3},{5,4},{6,5},{7,6},{0,7},{9,8},{10,9},{11,1... | collective-permute-start | bytes 393224 | tf_op jit(solution)/shard_map/ppermute | solution.py:18
  8.7 2.5 %copy-start.1 = (bf16[1,4,6,128,128]{4,3,2,1,0:T(8,128)(2,1)S(1)}, bf16[1,4,6,128,128]{4,3,2,1,0:T(8,128)(2,1)}, u32[]{:S(2)}) copy-start(bf16[1,4,6,128,128]{4,3,2,1,0:T(8,128)(2,1)} %param.17) | copy-start | bytes 2359300
  11.2 2.7 %copy-start.2 = (bf16[1,1,512,512]{3,2,1,0:T(8,128)(2,1)S(1)}, bf16[1,1,512,512]{3,2,1,0:T(8,128)(2,1)}, u32[]{:S(2)}) copy-start(bf16[1,1,512,512]{3,2,1,0:T(8,128)(2,1)} %param.12) | copy-start | bytes 1572868
  11.2 2.7 %copy-start.3 = (f32[512,512]{0,1:T(8,128)S(1)}, f32[512,512]{0,1:T(8,128)}, u32[]{:S(2)}) copy-start(f32[512,512]{0,1:T(8,128)} %fusion.81) | copy-start | bytes 3145732
  13.8 1.0 copy-start.29
  14.9 21.4 %copy-start.23 = (bf16[1,1,512,512]{3,2,1,0:T(8,128)(2,1)S(1)}, bf16[1,1,512,512]{3,2,1,0:T(8,128)(2,1)}, u32[]{:S(2)}) copy-start(bf16[1,1,512,512]{3,2,1,0:T(8,128)(2,1)} %param.10) | copy-start | bytes 1572868
  17.6 17.6 %collective-permute-start.2 = (bf16[512,512]{1,0:T(8,128)(2,1)}, bf16[512,512]{1,0:T(8,128)(2,1)S(1)}, u32[]{:S(2)}, u32[]{:S(2)}) collective-permute-start(bf16[512,512]{1,0:T(8,128)(2,1)} %fusion.7), channel_id=1, source_target_pairs={{0,8},{8,16},{16,24},{1,9},{9,17},{17,25},{2,10},{10,18},{18,26},{... | collective-permute-start | bytes 1572872 | tf_op jit(solution)/shard_map/ppermute | solution.py:28
  37.1 7.0 %collective-permute-start.3 = (bf16[128,512]{0,1:T(8,128)(2,1)S(1)}, bf16[128,512]{0,1:T(8,128)(2,1)S(1)}, u32[]{:S(2)}, u32[]{:S(2)}) collective-permute-start(bf16[128,512]{0,1:T(8,128)(2,1)S(1)} %get-tuple-element.15), channel_id=1, source_target_pairs={{0,1},{1,2},{2,3},{3,4},{4,5},{5,6},{6,7},{7,0},{8,9},{9,10},{10,1... | collective-permute-start | bytes 393224 | tf_op jit(solution)/shard_map/ppermute | solution.py:16
  37.3 6.8 %collective-permute-start.4 = (bf16[128,512]{0,1:T(8,128)(2,1)S(1)}, bf16[128,512]{0,1:T(8,128)(2,1)S(1)}, u32[]{:S(2)}, u32[]{:S(2)}) collective-permute-start(bf16[128,512]{0,1:T(8,128)(2,1)S(1)} %get-tuple-element.16), channel_id=1, source_target_pairs={{1,0},{2,1},{3,2},{4,3},{5,4},{6,5},{7,6},{0,7},{9,8},{10,9},{11,1... | collective-permute-start | bytes 393224 | tf_op jit(solution)/shard_map/ppermute | solution.py:18
  49.5 1.0 copy-start.7
  50.6 1.0 copy-start.30
  51.6 18.0 %copy-start.24 = (bf16[1,1,512,512]{3,2,1,0:T(8,128)(2,1)S(1)}, bf16[1,1,512,512]{3,2,1,0:T(8,128)(2,1)}, u32[]{:S(2)}) copy-start(bf16[1,1,512,512]{3,2,1,0:T(8,128)(2,1)} %param.10) | copy-start | bytes 1572868
  52.4 16.0 %collective-permute-start.5 = (bf16[512,512]{1,0:T(8,128)(2,1)S(1)}, bf16[512,512]{1,0:T(8,128)(2,1)S(1)}, u32[]{:S(2)}, u32[]{:S(2)}) collective-permute-start(bf16[512,512]{1,0:T(8,128)(2,1)S(1)} %add_convert_fusion.5), channel_id=1, source_target_pairs={{0,8},{8,16},{16,24},{1,9},{9,17},{17,25},{2,10},{10,18},{18,26},{... | collective-permute-start | bytes 1572872 | tf_op jit(solution)/shard_map/ppermute | solution.py:28
  70.4 6.2 %collective-permute-start.6 = (bf16[128,512]{0,1:T(8,128)(2,1)S(1)}, bf16[128,512]{0,1:T(8,128)(2,1)S(1)}, u32[]{:S(2)}, u32[]{:S(2)}) collective-permute-start(bf16[128,512]{0,1:T(8,128)(2,1)S(1)} %get-tuple-element.13), channel_id=1, source_target_pairs={{0,1},{1,2},{2,3},{3,4},{4,5},{5,6},{6,7},{7,0},{8,9},{9,10},{10,1... | collective-permute-start | bytes 393224 | tf_op jit(solution)/shard_map/ppermute | solution.py:16
  70.5 6.2 %collective-permute-start.7 = (bf16[128,512]{0,1:T(8,128)(2,1)S(1)}, bf16[128,512]{0,1:T(8,128)(2,1)S(1)}, u32[]{:S(2)}, u32[]{:S(2)}) collective-permute-start(bf16[128,512]{0,1:T(8,128)(2,1)S(1)} %get-tuple-element.14), channel_id=1, source_target_pairs={{1,0},{2,1},{3,2},{4,3},{5,4},{6,5},{7,6},{0,7},{9,8},{10,9},{11,1... | collective-permute-start | bytes 393224 | tf_op jit(solution)/shard_map/ppermute | solution.py:18
  82.0 1.0 copy-start.9
  83.0 1.0 copy-start.31
  84.1 16.3 %copy-start.25 = (bf16[1,1,512,512]{3,2,1,0:T(8,128)(2,1)S(1)}, bf16[1,1,512,512]{3,2,1,0:T(8,128)(2,1)}, u32[]{:S(2)}) copy-start(bf16[1,1,512,512]{3,2,1,0:T(8,128)(2,1)} %param.10) | copy-start | bytes 1572868
  84.9 14.4 %collective-permute-start.8 = (bf16[512,512]{1,0:T(8,128)(2,1)S(1)}, bf16[512,512]{1,0:T(8,128)(2,1)S(1)}, u32[]{:S(2)}, u32[]{:S(2)}) collective-permute-start(bf16[512,512]{1,0:T(8,128)(2,1)S(1)} %add_convert_fusion.4), channel_id=1, source_target_pairs={{0,8},{8,16},{16,24},{1,9},{9,17},{17,25},{2,10},{10,18},{18,26},{... | collective-permute-start | bytes 1572872 | tf_op jit(solution)/shard_map/ppermute | solution.py:28
  101.2 6.2 %collective-permute-start.9 = (bf16[128,512]{0,1:T(8,128)(2,1)S(1)}, bf16[128,512]{0,1:T(8,128)(2,1)S(1)}, u32[]{:S(2)}, u32[]{:S(2)}) collective-permute-start(bf16[128,512]{0,1:T(8,128)(2,1)S(1)} %get-tuple-element.11), channel_id=1, source_target_pairs={{0,1},{1,2},{2,3},{3,4},{4,5},{5,6},{6,7},{7,0},{8,9},{9,10},{10,1... | collective-permute-start | bytes 393224 | tf_op jit(solution)/shard_map/ppermute | solution.py:16
  101.3 6.2 %collective-permute-start.10 = (bf16[128,512]{0,1:T(8,128)(2,1)S(1)}, bf16[128,512]{0,1:T(8,128)(2,1)S(1)}, u32[]{:S(2)}, u32[]{:S(2)}) collective-permute-start(bf16[128,512]{0,1:T(8,128)(2,1)S(1)} %get-tuple-element.12), channel_id=1, source_target_pairs={{1,0},{2,1},{3,2},{4,3},{5,4},{6,5},{7,6},{0,7},{9,8},{10,9},{11,1... | collective-permute-start | bytes 393224 | tf_op jit(solution)/shard_map/ppermute | solution.py:18
  112.8 1.0 copy-start.11
  113.9 1.0 copy-start.32
  114.9 16.9 %copy-start.26 = (bf16[1,1,512,512]{3,2,1,0:T(8,128)(2,1)S(1)}, bf16[1,1,512,512]{3,2,1,0:T(8,128)(2,1)}, u32[]{:S(2)}) copy-start(bf16[1,1,512,512]{3,2,1,0:T(8,128)(2,1)} %param.10) | copy-start | bytes 1572868
  115.7 1.9 copy-start.16
  115.8 14.9 %collective-permute-start.11 = (bf16[512,512]{1,0:T(8,128)(2,1)S(1)}, bf16[512,512]{1,0:T(8,128)(2,1)S(1)}, u32[]{:S(2)}, u32[]{:S(2)}) collective-permute-start(bf16[512,512]{1,0:T(8,128)(2,1)S(1)} %add_convert_fusion.3), channel_id=1, source_target_pairs={{0,8},{8,16},{16,24},{1,9},{9,17},{17,25},{2,10},{10,18},{18,26},{... | collective-permute-start | bytes 1572872 | tf_op jit(solution)/shard_map/ppermute | solution.py:28
  132.6 6.3 %collective-permute-start.12 = (bf16[128,512]{0,1:T(8,128)(2,1)S(1)}, bf16[128,512]{0,1:T(8,128)(2,1)S(1)}, u32[]{:S(2)}, u32[]{:S(2)}) collective-permute-start(bf16[128,512]{0,1:T(8,128)(2,1)S(1)} %get-tuple-element.9), channel_id=1, source_target_pairs={{0,1},{1,2},{2,3},{3,4},{4,5},{5,6},{6,7},{7,0},{8,9},{9,10},{10,1... | collective-permute-start | bytes 393224 | tf_op jit(solution)/shard_map/ppermute | solution.py:16
  132.7 6.3 %collective-permute-start.13 = (bf16[128,512]{0,1:T(8,128)(2,1)S(1)}, bf16[128,512]{0,1:T(8,128)(2,1)S(1)}, u32[]{:S(2)}, u32[]{:S(2)}) collective-permute-start(bf16[128,512]{0,1:T(8,128)(2,1)S(1)} %get-tuple-element.10), channel_id=1, source_target_pairs={{1,0},{2,1},{3,2},{4,3},{5,4},{6,5},{7,6},{0,7},{9,8},{10,9},{11,1... | collective-permute-start | bytes 393224 | tf_op jit(solution)/shard_map/ppermute | solution.py:18
  144.3 1.0 copy-start.13
  145.4 1.0 copy-start.33
  146.4 18.6 %copy-start.27 = (bf16[1,1,512,512]{3,2,1,0:T(8,128)(2,1)S(1)}, bf16[1,1,512,512]{3,2,1,0:T(8,128)(2,1)}, u32[]{:S(2)}) copy-start(bf16[1,1,512,512]{3,2,1,0:T(8,128)(2,1)} %param.10) | copy-start | bytes 1572868
  147.3 1.9 copy-start.18
  147.3 16.7 %collective-permute-start.14 = (bf16[512,512]{1,0:T(8,128)(2,1)S(1)}, bf16[512,512]{1,0:T(8,128)(2,1)S(1)}, u32[]{:S(2)}, u32[]{:S(2)}) collective-permute-start(bf16[512,512]{1,0:T(8,128)(2,1)S(1)} %add_convert_fusion.2), channel_id=1, source_target_pairs={{0,8},{8,16},{16,24},{1,9},{9,17},{17,25},{2,10},{10,18},{18,26},{... | collective-permute-start | bytes 1572872 | tf_op jit(solution)/shard_map/ppermute | solution.py:28
  165.9 6.2 %collective-permute-start.15 = (bf16[128,512]{0,1:T(8,128)(2,1)S(1)}, bf16[128,512]{0,1:T(8,128)(2,1)S(1)}, u32[]{:S(2)}, u32[]{:S(2)}) collective-permute-start(bf16[128,512]{0,1:T(8,128)(2,1)S(1)} %get-tuple-element.7), channel_id=1, source_target_pairs={{0,1},{1,2},{2,3},{3,4},{4,5},{5,6},{6,7},{7,0},{8,9},{9,10},{10,1... | collective-permute-start | bytes 393224 | tf_op jit(solution)/shard_map/ppermute | solution.py:16
  165.9 6.2 %collective-permute-start.16 = (bf16[128,512]{0,1:T(8,128)(2,1)S(1)}, bf16[128,512]{0,1:T(8,128)(2,1)S(1)}, u32[]{:S(2)}, u32[]{:S(2)}) collective-permute-start(bf16[128,512]{0,1:T(8,128)(2,1)S(1)} %get-tuple-element.8), channel_id=1, source_target_pairs={{1,0},{2,1},{3,2},{4,3},{5,4},{6,5},{7,6},{0,7},{9,8},{10,9},{11,1... | collective-permute-start | bytes 393224 | tf_op jit(solution)/shard_map/ppermute | solution.py:18
  177.5 1.0 copy-start.15
  179.6 16.0 %copy-start.28 = (bf16[1,1,512,512]{3,2,1,0:T(8,128)(2,1)S(1)}, bf16[1,1,512,512]{3,2,1,0:T(8,128)(2,1)}, u32[]{:S(2)}) copy-start(bf16[1,1,512,512]{3,2,1,0:T(8,128)(2,1)} %param.10) | copy-start | bytes 1572868
  180.4 1.9 copy-start.20
  180.4 14.1 %collective-permute-start.17 = (bf16[512,512]{1,0:T(8,128)(2,1)S(1)}, bf16[512,512]{1,0:T(8,128)(2,1)S(1)}, u32[]{:S(2)}, u32[]{:S(2)}) collective-permute-start(bf16[512,512]{1,0:T(8,128)(2,1)S(1)} %add_convert_fusion.1), channel_id=1, source_target_pairs={{0,8},{8,16},{16,24},{1,9},{9,17},{17,25},{2,10},{10,18},{18,26},{... | collective-permute-start | bytes 1572872 | tf_op jit(solution)/shard_map/ppermute | solution.py:28
  196.4 6.3 %collective-permute-start.18 = (bf16[128,512]{0,1:T(8,128)(2,1)S(1)}, bf16[128,512]{0,1:T(8,128)(2,1)S(1)}, u32[]{:S(2)}, u32[]{:S(2)}) collective-permute-start(bf16[128,512]{0,1:T(8,128)(2,1)S(1)} %get-tuple-element.5), channel_id=1, source_target_pairs={{0,1},{1,2},{2,3},{3,4},{4,5},{5,6},{6,7},{7,0},{8,9},{9,10},{10,1... | collective-permute-start | bytes 393224 | tf_op jit(solution)/shard_map/ppermute | solution.py:16
  196.5 6.3 %collective-permute-start.19 = (bf16[128,512]{0,1:T(8,128)(2,1)S(1)}, bf16[128,512]{0,1:T(8,128)(2,1)S(1)}, u32[]{:S(2)}, u32[]{:S(2)}) collective-permute-start(bf16[128,512]{0,1:T(8,128)(2,1)S(1)} %get-tuple-element.6), channel_id=1, source_target_pairs={{1,0},{2,1},{3,2},{4,3},{5,4},{6,5},{7,6},{0,7},{9,8},{10,9},{11,1... | collective-permute-start | bytes 393224 | tf_op jit(solution)/shard_map/ppermute | solution.py:18
  208.1 1.0 copy-start.5
  210.2 1.2 copy-start.19
  210.2 1.4 copy-start.21
  (10 other events, 8.9 us)
where the time goes:
time: 244 us; the launch traced here: 241 us
  waiting for transfers between devices  96.7 us (40%)
  matrix products  39.8 us (16%)
  starting transfers between devices  39 us (16%)
  local copies, waits for them, and re-layouts  28 us (11%)
  blocking collectives  25.9 us (11%)
  other arithmetic  10.4 us (4%)
    ppermute x6, waiting for transfers between devices, from_behind(): return lax.ppermute(shard, axis, pairs)  79.8 us
    all_to_all x1, blocking collectives, shards(): lax.all_to_all(kept, 'segment', split_axis=0, concat_axis=0, tiled=True)  25.9 us
    ppermute x7, starting transfers between devices, extended(): lax.ppermute(head, axis, [((i + 1) % count, i) for i in range(count)])  24.6 us
    dot_general x7, matrix products, run_layer(): jnp.einsum('bkij,bkjd->bid', weights, picked, preferred_element_type=jnp....  17.7 us
    gather x7, local copies, waits for them, and re-layouts, run_layer(): picked = padded_blocks[local_index]  17.4 us
    ppermute x7, waiting for transfers between devices, extended(): lax.ppermute(tail, axis, [(i, (i + 1) % count) for i in range(count)])  16.9 us
    ppermute x6, starting transfers between devices, from_behind(): return lax.ppermute(shard, axis, pairs)  13.8 us
    unnamed x76, local copies, waits for them, and re-layouts  8.43 us
  transfers between devices with their start and end apart: 20, of which 13 were waited for; matrix products, arithmetic and copies ran while one was open for 1% of the time, Pallas kernels for 0%

commit v1 on v0

v1 whole, which is shorter than its diff:
```python
import jax
import jax.numpy as jnp
from jax import lax
from jax.sharding import PartitionSpec as P

HB = 1


def from_neighbours(cells, width):
    count = lax.axis_size("dom")
    head = cells[:width]
    tail = cells[cells.shape[0] - width :]
    before = lax.ppermute(tail, "dom", [(i, (i + 1) % count) for i in range(count)])
    after = lax.ppermute(head, "dom", [((i + 1) % count, i) for i in range(count)])
    return before, after


def dense_edges(sources, counts, tiles):
    blocks, slots, rows, _ = tiles.shape
    window = blocks + 2 * HB
    total = blocks * lax.axis_size("dom")
    first = lax.axis_index("dom") * blocks - HB
    local = jnp.mod(sources - first, total)
    used = jnp.arange(slots, dtype=jnp.int32)[None, :] < counts[:, None]
    hits = (local[:, :, None] == jnp.arange(window, dtype=jnp.int32)) & used[:, :, None]
    dense = jnp.sum(
        jnp.where(hits[:, :, None, :, None], tiles[:, :, :, None, :].astype(jnp.float32), 0.0),
        axis=1,
    )
    return dense.reshape(blocks * rows, window * rows).astype(jnp.bfloat16)


def shards(
    samples, w_source, w_self, w_message, w_output, norm_gain, tile_source, tile_count, tile_value
):
    sections = lax.axis_size("segment")
    mine = lax.axis_index("segment")
    edges = dense_edges(tile_source[0], tile_count[0], tile_value[0])
    halo = HB * tile_value.shape[-1]
    weights = jnp.concatenate([w_source[0, 0], w_self[0, 0], w_message[0, 0], w_output[0, 0]])
    weights = lax.all_gather(weights, "segment")
    edges = lax.all_gather(edges, "segment")
    gains = lax.all_gather(norm_gain[0, 0], "segment")
    h = lax.dynamic_index_in_dim(samples, mine, 0, keepdims=False)
    width = h.shape[1]
    for s in range(sections):
        wa, wb, wc, wd = (weights[s, i * width : (i + 1) * width] for i in range(4))
        sender = jax.nn.silu(jnp.dot(h, wa, preferred_element_type=jnp.float32)).astype(
            jnp.bfloat16
        )
        before, after = from_neighbours(sender, halo)
        padded = jnp.concatenate([before, sender, after])
        gathered = jnp.dot(edges[s], padded, preferred_element_type=jnp.float32).astype(
            jnp.bfloat16
        )
        mixed = jnp.dot(h, wb, preferred_element_type=jnp.float32) + jnp.dot(
            gathered, wc, preferred_element_type=jnp.float32
        )
        scale = lax.rsqrt(jnp.mean(mixed * mixed, axis=-1, keepdims=True) + 1e-05)
        update = jax.nn.silu(mixed * scale * gains[s]).astype(jnp.bfloat16)
        h = (
            h.astype(jnp.float32) + jnp.dot(update, wd, preferred_element_type=jnp.float32)
        ).astype(jnp.bfloat16)
    return h[None]


def solution(mesh):
    return jax.shard_map(
        shards,
        mesh=mesh,
        in_specs=(
            P(None, "dom", None),
            P("segment", None, None, None),
            P("segment", None, None, None),
            P("segment", None, None, None),
            P("segment", None, None, None),
            P("segment", None, None),
            P("segment", "dom", None),
            P("segment", "dom"),
            P("segment", "dom", None, None, None),
        ),
        out_specs=P("segment", "dom", None),
        check_vma=False,
    )
```

time: 244 us -> 200 us (0.82)
  starting transfers between devices: 39 us -> 13.7 us
  local copies, waits for them, and re-layouts: 28 us -> 3.13 us
  waiting for transfers between devices: 96.7 us -> 121 us
  blocking collectives: 25.9 us -> 8.07 us
  between operations: 0.79 us -> 13.7 us
  matrix products: 39.8 us -> 32.9 us
  other arithmetic: 10.4 us -> 4.53 us
    all_gather x0 -> x2, waiting for transfers between devices: none -> 116 us  [the longest x1 76.9 us: shards(): weights = lax.all_gather(weights, 'segment')]
    ppermute x20 -> x8, waiting for transfers between devices: 96.7 us -> 5.56 us  [the longest x4 5.55 us: from_neighbours(): lax.ppermute(tail, 'dom', [(i, (i + 1) % count) for i in range(count)])]
    all_to_all x1 -> x0, blocking collectives: 25.9 us -> none  [shards(): lax.all_to_all(kept, 'segment', split_axis=0, concat_axis=0, tiled=True)]
    ppermute x20 -> x8, starting transfers between devices: 39 us -> 13.7 us  [the longest x4 12.3 us: from_neighbours(): lax.ppermute(head, 'dom', [((i + 1) % count, i) for i in range(count)])]
    gather x7 -> x0, local copies, waits for them, and re-layouts: 17.4 us -> none  [run_layer(): picked = padded_blocks[local_index]]
    all_gather x0 -> x1, blocking collectives: none -> 8.07 us  [shards(): gains = lax.all_gather(norm_gain[0, 0], 'segment')]
    unnamed x76 -> x12, local copies, waits for them, and re-layouts: 8.43 us -> 0.72 us
    dot_general x35 -> x16, matrix products: 39.8 us -> 32.9 us  [the longest x4 11.3 us: shards(): jnp.dot(gathered, wc, preferred_element_type=jnp.float32)]
  transfers between devices with their start and end apart: 20 -> 10, of which waited for: 13 -> 5; matrix products, arithmetic and copies ran while one was open for 1% -> 6% of each run, Pallas kernels for 0% -> 0%
where the time goes in v1:
time: 200 us; the launch traced here: 197 us
  waiting for transfers between devices  121 us (60%)
  matrix products  32.9 us (16%)
  starting transfers between devices  13.7 us (7%)
  between operations  13.7 us (7%)
  blocking collectives  8.07 us (4%)
  other arithmetic  4.53 us (2%)
  local copies, waits for them, and re-layouts  3.13 us (2%)
    all_gather x1, waiting for transfers between devices, shards(): weights = lax.all_gather(weights, 'segment')  76.9 us
    all_gather x1, waiting for transfers between devices, shards(): edges = lax.all_gather(edges, 'segment')  38.9 us
    ppermute x4, starting transfers between devices, from_neighbours(): lax.ppermute(head, 'dom', [((i + 1) % count, i) for i in range(count)])  12.3 us
    dot_general x4, matrix products, shards(): jnp.dot(gathered, wc, preferred_element_type=jnp.float32)  11.3 us
    dot_general x4, matrix products, shards(): jnp.dot(update, wd, preferred_element_type=jnp.float32)  8.81 us
    all_gather x1, blocking collectives, shards(): gains = lax.all_gather(norm_gain[0, 0], 'segment')  8.07 us
    dot_general x4, matrix products, shards(): jnp.dot(h, wa, preferred_element_type=jnp.float32)  6.69 us
    dot_general x4, matrix products, shards(): jnp.dot(h, wb, preferred_element_type=jnp.float32)  6.09 us
  transfers between devices with their start and end apart: 10, of which 5 were waited for; matrix products, arithmetic and copies ran while one was open for 6% of the time, Pallas kernels for 0%

profile of v1, /device:TPU:4, one launch (start us, length us, event | category | flops | bytes accessed | tf_op | source)
XLA Modules:
  0.0 197.4 jit_solution(4902868587040868669)
XLA Ops:
  6.5 3.2 %pad_maximum_fusion = bf16[2048,512]{1,0:T(8,128)(2,1)} fusion(bf16[512,512]{1,0:T(8,128)(2,1)} %bitcast.135, bf16[512,512]{1,0:T(8,128)(2,1)} %bitcast.136, bf16[512,512]{1,0:T(8,128)(2,1)} %bitcast.137, bf16[512,512]{1,0:T(8,128)(2,1)} %bitcast.138), kind=kLoop, calls=%fused_computation.1 | loop fusion | flops 8388608 | bytes 4194304 | tf_op jit(solution)/shard_map/concatenate | solution.py:40
  9.7 0.0 all-gather.7.cloned.1.call-update
  9.7 0.0 all-gather.5.cloned.1.call-start
  9.8 0.1 iota_compare_fusion.1
  9.9 0.1 fusion.69
  10.0 0.2 bitcast_convert_fusion
  10.2 0.0 copy-start.3
  10.2 0.0 copy-start.1
  10.2 1.0 select_reduce_fusion
  11.2 0.5 copy.49
  11.7 1.8 reshape.110
  13.5 0.0 all-gather.5.cloned.1.call-update
  13.6 8.1 %all-gather.1 = f32[4,1,512]{2,1,0:T(1,128)S(1)} all-gather(f32[1,1,512]{2,1,0:T(1,128)S(1)} %copy-done.3), channel_id=3, replica_groups=mesh['segment'=4,'dom'=8] {'segment'}, dimensions={0}, use_global_device_ids=true | all-gather | bytes 10240 | tf_op jit(solution)/shard_map/all_gather | solution.py:43
  21.6 76.9 %all-gather.7.cloned.1.call-done = bf16[8192,512]{1,0:T(8,128)(2,1)} async-done(((bf16[2048,512]{1,0:T(8,128)(2,1)}), bf16[8192,512]{1,0:T(8,128)(2,1)}) %all-gather.7.cloned.1.call-update) | async-done | bytes 8388624 | tf_op jit(solution)/shard_map/all_gather | solution.py:41
  98.6 1.7 multiply_convert_fusion.7
  100.3 0.0 copy-start.2
  100.3 0.1 collective-permute-start
  100.4 0.7 copy-done.2
  101.1 2.8 %collective-permute-start.1 = (bf16[128,512]{0,1:T(8,128)(2,1)S(1)}, bf16[128,512]{0,1:T(8,128)(2,1)}, u32[]{:S(2)}, u32[]{:S(2)}) collective-permute-start(bf16[128,512]{0,1:T(8,128)(2,1)S(1)} %get-tuple-element.12), channel_id=1, source_target_pairs={{1,0},{2,1},{3,2},{4,3},{5,4},{6,5},{7,6},{0,7},{9,8},{10,9},{11,1... | collective-permute-start | bytes 393224 | tf_op jit(solution)/shard_map/ppermute | solution.py:14
  103.9 1.5 fusion.52
  105.4 38.9 %all-gather.5.cloned.1.call-done = bf16[4,512,768]{2,1,0:T(8,128)(2,1)} async-done(((bf16[1,512,768]{2,1,0:T(8,128)(2,1)}), bf16[4,512,768]{2,1,0:T(8,128)(2,1)}) %all-gather.5.cloned.1.call-update) | async-done | bytes 3145744 | tf_op jit(solution)/shard_map/all_gather | solution.py:42
  144.3 0.0 collective-permute-done
  144.3 0.0 collective-permute-done.1
  144.3 3.5 %multiply_reduce_fusion.3 = (f32[512]{0:T(512)S(1)}, f32[512,512]{0,1:T(8,128)}) fusion(f32[512,512]{0,1:T(8,128)S(1)} %fusion.52, bf16[4,2048,512]{2,1,0:T(8,128)(2,1)} %bitcast.121, bf16[4,512,768]{2,1,0:T(8,128)(2,1)} %all-gather.5.cloned.1.call-done, bf16[128,512]{0,1:T(8,128)(2,1)} %collective-permute-done.1, bf16[512,512]{0,1:T(8,128)(2,1)} %copy-done.2, ...), kind=kOutput, calls=%fused_computation.29 | convolution fusion | flops 674496000 | bytes 4196352 | tf_op jit(solution)/shard_map/dot_general | solution.py:56
  147.8 2.2 %fusion = bf16[512,512]{1,0:T(8,128)(2,1)S(1)} fusion(f32[512,512]{0,1:T(8,128)} %get-tuple-element.18, bf16[4,2048,512]{2,1,0:T(8,128)(2,1)} %bitcast.122, f32[512]{0:T(512)S(1)} %bitcast.142, f32[512]{0:T(512)S(1)} %add_rsqrt_fusion.3, bf16[4,512,512]{2,1,0:T(8,128)(2,1)S(1)} %copy-done.1, s32[]{:T(128)S(6)} %select_n.19), kind=kOutput, calls=%fused_computation.14 | convolution fusion | flops 271056896 | bytes 2625540 | tf_op jit(solution)/shard_map/dot_general | solution.py:62
  149.9 1.7 multiply_convert_fusion.5
  151.6 0.1 collective-permute-start.2
  151.7 3.5 %collective-permute-start.3 = (bf16[128,512]{0,1:T(8,128)(2,1)S(1)}, bf16[128,512]{0,1:T(8,128)(2,1)S(1)}, u32[]{:S(2)}, u32[]{:S(2)}) collective-permute-start(bf16[128,512]{0,1:T(8,128)(2,1)S(1)} %get-tuple-element.10), channel_id=1, source_target_pairs={{1,0},{2,1},{3,2},{4,3},{5,4},{6,5},{7,6},{0,7},{9,8},{10,9},{11,1... | collective-permute-start | bytes 393224 | tf_op jit(solution)/shard_map/ppermute | solution.py:14
  155.2 1.5 fusion.50
  156.8 1.2 collective-permute-done.2
  158.0 0.0 collective-permute-done.3
  158.0 3.3 %multiply_reduce_fusion.2 = (f32[512]{0:T(512)S(1)}, f32[512,512]{0,1:T(8,128)}) fusion(f32[512,512]{0,1:T(8,128)S(1)} %fusion.50, bf16[4,2048,512]{2,1,0:T(8,128)(2,1)} %bitcast.125, bf16[4,512,768]{2,1,0:T(8,128)(2,1)} %all-gather.5.cloned.1.call-done, bf16[128,512]{0,1:T(8,128)(2,1)S(1)} %collective-permute-done.3, ...), kind=kOutput, calls=%fused_computation.26 | convolution fusion | flops 674496000 | bytes 4196352 | tf_op jit(solution)/shard_map/dot_general | solution.py:56
  161.3 2.2 %fusion.1 = bf16[512,512]{1,0:T(8,128)(2,1)S(1)} fusion(bf16[512,512]{1,0:T(8,128)(2,1)S(1)} %fusion, f32[512,512]{0,1:T(8,128)} %get-tuple-element.20, bf16[4,2048,512]{2,1,0:T(8,128)(2,1)} %bitcast.126, f32[512]{0:T(512)S(1)} %bitcast.141, f32[512]{0:T(512)S(1)} %add_rsqrt_fusion.2), kind=kOutput, calls=%fused_computation.15 | convolution fusion | flops 271056896 | bytes 2625536 | tf_op jit(solution)/shard_map/dot_general | solution.py:62
  163.4 1.7 multiply_convert_fusion.3
  165.2 1.2 collective-permute-start.4
  166.3 2.4 %collective-permute-start.5 = (bf16[128,512]{0,1:T(8,128)(2,1)S(1)}, bf16[128,512]{0,1:T(8,128)(2,1)S(1)}, u32[]{:S(2)}, u32[]{:S(2)}) collective-permute-start(bf16[128,512]{0,1:T(8,128)(2,1)S(1)} %get-tuple-element.8), channel_id=1, source_target_pairs={{1,0},{2,1},{3,2},{4,3},{5,4},{6,5},{7,6},{0,7},{9,8},{10,9},{11,1... | collective-permute-start | bytes 393224 | tf_op jit(solution)/shard_map/ppermute | solution.py:14
  168.7 1.5 fusion.48
  170.3 1.9 collective-permute-done.4
  172.2 0.0 collective-permute-done.5
  172.2 2.3 %multiply_reduce_fusion.1 = (f32[512]{0:T(512)S(1)}, f32[512,512]{0,1:T(8,128)S(1)}) fusion(f32[512,512]{0,1:T(8,128)S(1)} %fusion.48, bf16[4,2048,512]{2,1,0:T(8,128)(2,1)} %bitcast.129, bf16[4,512,768]{2,1,0:T(8,128)(2,1)} %all-gather.5.cloned.1.call-done, bf16[128,512]{0,1:T(8,128)(2,1)S(1)} %collective-permute-done.5, ...), kind=kOutput, calls=%fused_computation.23 | convolution fusion | flops 674496000 | bytes 4196352 | tf_op jit(solution)/shard_map/dot_general | solution.py:56
  174.5 1.9 fusion.2
  176.4 1.7 multiply_convert_fusion.1
  178.1 0.2 collective-permute-start.6
  178.3 3.4 %collective-permute-start.7 = (bf16[128,512]{0,1:T(8,128)(2,1)S(1)}, bf16[128,512]{0,1:T(8,128)(2,1)S(1)}, u32[]{:S(2)}, u32[]{:S(2)}) collective-permute-start(bf16[128,512]{0,1:T(8,128)(2,1)S(1)} %get-tuple-element.6), channel_id=1, source_target_pairs={{1,0},{2,1},{3,2},{4,3},{5,4},{6,5},{7,6},{0,7},{9,8},{10,9},{11,1... | collective-permute-start | bytes 393224 | tf_op jit(solution)/shard_map/ppermute | solution.py:14
  181.7 1.5 fusion.46
  183.2 2.4 %collective-permute-done.6 = bf16[128,512]{0,1:T(8,128)(2,1)S(1)} collective-permute-done((bf16[128,512]{0,1:T(8,128)(2,1)S(1)}, bf16[128,512]{0,1:T(8,128)(2,1)S(1)}, u32[]{:S(2)}, u32[]{:S(2)}) %collective-permute-start.6) | collective-permute-done | bytes 131104 | tf_op jit(solution)/shard_map/ppermute | solution.py:13
  185.6 2.3 %multiply_reduce_fusion = (f32[512]{0:T(512)S(1)}, f32[512,512]{0,1:T(8,128)S(1)}) fusion(f32[512,512]{0,1:T(8,128)S(1)} %fusion.46, bf16[4,2048,512]{2,1,0:T(8,128)(2,1)} %bitcast.133, bf16[4,512,768]{2,1,0:T(8,128)(2,1)} %all-gather.5.cloned.1.call-done, bf16[128,512]{0,1:T(8,128)(2,1)S(1)} %collective-permute-done.7, ...), kind=kOutput, calls=%fused_computation.20 | convolution fusion | flops 674496000 | bytes 4196352 | tf_op jit(solution)/shard_map/dot_general | solution.py:56
  187.9 2.6 %fusion.4 = bf16[1,512,512]{2,1,0:T(8,128)(2,1)} fusion(bf16[512,512]{1,0:T(8,128)(2,1)S(1)} %fusion.2, f32[512,512]{0,1:T(8,128)S(1)} %get-tuple-element.24, bf16[4,2048,512]{2,1,0:T(8,128)(2,1)} %bitcast.134, f32[512]{0:T(512)S(1)} %bitcast.139, f32[512]{0:T(512)S(1)} %add_rsqrt_fusion), kind=kOutput, calls=%fused_computation.18 | convolution fusion | flops 271056896 | bytes 2625536 | tf_op jit(solution)/shard_map/dot_general | solution.py:62
  (20 shorter events, 0.1 us)
Async XLA Ops:
  6.5 92.0 %all-gather.7.cloned.1.call-start = ((), (), s32[]{:S(2)}) async-start(), calls=%async_computation.1 | async-start | bytes 10485760 | tf_op jit(solution)/shard_map/all_gather | solution.py:41
  6.5 3.3 %copy-start.5 = (s32[1,4]{1,0:T(1,128)S(1)}, s32[1,4]{1,0:T(1,128)}, u32[]{:S(2)}) copy-start(s32[1,4]{1,0:T(1,128)} %param.16) | copy-start | bytes 52
  6.5 3.4 %copy-start.4 = (s32[1,4,6]{2,1,0:T(4,128)S(1)}, s32[1,4,6]{2,1,0:T(4,128)}, u32[]{:S(2)}) copy-start(s32[1,4,6]{2,1,0:T(4,128)} %param.15) | copy-start | bytes 292
  6.5 3.4 %copy-start = (bf16[1,4,6,128,128]{4,3,2,1,0:T(8,128)(2,1)S(1)}, bf16[1,4,6,128,128]{4,3,2,1,0:T(8,128)(2,1)}, u32[]{:S(2)}) copy-start(bf16[1,4,6,128,128]{4,3,2,1,0:T(8,128)(2,1)} %param.17) | copy-start | bytes 2359300
  9.7 134.5 %all-gather.5.cloned.1.call-start = ((), (), s32[]{:S(2)}) async-start(), calls=%async_computation | async-start | bytes 3932160 | tf_op jit(solution)/shard_map/all_gather | solution.py:42
  10.2 3.4 %copy-start.3 = (f32[1,1,512]{2,1,0:T(1,128)S(1)}, f32[1,1,512]{2,1,0:T(1,128)}, u32[]{:S(2)}) copy-start(f32[1,1,512]{2,1,0:T(1,128)} %param.14) | copy-start | bytes 6148
  10.2 88.4 %copy-start.1 = (bf16[4,512,512]{2,1,0:T(8,128)(2,1)S(1)}, bf16[4,512,512]{2,1,0:T(8,128)(2,1)}, u32[]{:S(2)}) copy-start(bf16[4,512,512]{2,1,0:T(8,128)(2,1)} %param.9) | copy-start | bytes 6291460
  100.3 0.8 copy-start.2
  100.3 44.0 %collective-permute-start = (bf16[128,512]{0,1:T(8,128)(2,1)S(1)}, bf16[128,512]{0,1:T(8,128)(2,1)S(1)}, u32[]{:S(2)}, u32[]{:S(2)}) collective-permute-start(bf16[128,512]{0,1:T(8,128)(2,1)S(1)} %get-tuple-element.11), channel_id=1, source_target_pairs={{0,1},{1,2},{2,3},{3,4},{4,5},{5,6},{6,7},{7,0},{8,9},{9,10},{10,1... | collective-permute-start | bytes 393224 | tf_op jit(solution)/shard_map/ppermute | solution.py:13
  101.1 43.2 %collective-permute-start.1 = (bf16[128,512]{0,1:T(8,128)(2,1)S(1)}, bf16[128,512]{0,1:T(8,128)(2,1)}, u32[]{:S(2)}, u32[]{:S(2)}) collective-permute-start(bf16[128,512]{0,1:T(8,128)(2,1)S(1)} %get-tuple-element.12), channel_id=1, source_target_pairs={{1,0},{2,1},{3,2},{4,3},{5,4},{6,5},{7,6},{0,7},{9,8},{10,9},{11,1... | collective-permute-start | bytes 393224 | tf_op jit(solution)/shard_map/ppermute | solution.py:14
  151.6 6.3 %collective-permute-start.2 = (bf16[128,512]{0,1:T(8,128)(2,1)S(1)}, bf16[128,512]{0,1:T(8,128)(2,1)S(1)}, u32[]{:S(2)}, u32[]{:S(2)}) collective-permute-start(bf16[128,512]{0,1:T(8,128)(2,1)S(1)} %get-tuple-element.9), channel_id=1, source_target_pairs={{0,1},{1,2},{2,3},{3,4},{4,5},{5,6},{6,7},{7,0},{8,9},{9,10},{10,1... | collective-permute-start | bytes 393224 | tf_op jit(solution)/shard_map/ppermute | solution.py:13
  151.7 6.3 %collective-permute-start.3 = (bf16[128,512]{0,1:T(8,128)(2,1)S(1)}, bf16[128,512]{0,1:T(8,128)(2,1)S(1)}, u32[]{:S(2)}, u32[]{:S(2)}) collective-permute-start(bf16[128,512]{0,1:T(8,128)(2,1)S(1)} %get-tuple-element.10), channel_id=1, source_target_pairs={{1,0},{2,1},{3,2},{4,3},{5,4},{6,5},{7,6},{0,7},{9,8},{10,9},{11,1... | collective-permute-start | bytes 393224 | tf_op jit(solution)/shard_map/ppermute | solution.py:14
  165.2 7.1 %collective-permute-start.4 = (bf16[128,512]{0,1:T(8,128)(2,1)S(1)}, bf16[128,512]{0,1:T(8,128)(2,1)S(1)}, u32[]{:S(2)}, u32[]{:S(2)}) collective-permute-start(bf16[128,512]{0,1:T(8,128)(2,1)S(1)} %get-tuple-element.7), channel_id=1, source_target_pairs={{0,1},{1,2},{2,3},{3,4},{4,5},{5,6},{6,7},{7,0},{8,9},{9,10},{10,1... | collective-permute-start | bytes 393224 | tf_op jit(solution)/shard_map/ppermute | solution.py:13
  166.3 5.9 %collective-permute-start.5 = (bf16[128,512]{0,1:T(8,128)(2,1)S(1)}, bf16[128,512]{0,1:T(8,128)(2,1)S(1)}, u32[]{:S(2)}, u32[]{:S(2)}) collective-permute-start(bf16[128,512]{0,1:T(8,128)(2,1)S(1)} %get-tuple-element.8), channel_id=1, source_target_pairs={{1,0},{2,1},{3,2},{4,3},{5,4},{6,5},{7,6},{0,7},{9,8},{10,9},{11,1... | collective-permute-start | bytes 393224 | tf_op jit(solution)/shard_map/ppermute | solution.py:14
  178.1 7.5 %collective-permute-start.6 = (bf16[128,512]{0,1:T(8,128)(2,1)S(1)}, bf16[128,512]{0,1:T(8,128)(2,1)S(1)}, u32[]{:S(2)}, u32[]{:S(2)}) collective-permute-start(bf16[128,512]{0,1:T(8,128)(2,1)S(1)} %get-tuple-element.5), channel_id=1, source_target_pairs={{0,1},{1,2},{2,3},{3,4},{4,5},{5,6},{6,7},{7,0},{8,9},{9,10},{10,1... | collective-permute-start | bytes 393224 | tf_op jit(solution)/shard_map/ppermute | solution.py:13
  178.3 7.4 %collective-permute-start.7 = (bf16[128,512]{0,1:T(8,128)(2,1)S(1)}, bf16[128,512]{0,1:T(8,128)(2,1)S(1)}, u32[]{:S(2)}, u32[]{:S(2)}) collective-permute-start(bf16[128,512]{0,1:T(8,128)(2,1)S(1)} %get-tuple-element.6), channel_id=1, source_target_pairs={{1,0},{2,1},{3,2},{4,3},{5,4},{6,5},{7,6},{0,7},{9,8},{10,9},{11,1... | collective-permute-start | bytes 393224 | tf_op jit(solution)/shard_map/ppermute | solution.py:14
Sparse Core Ops, SparseCore 0:
  9.9 88.6 all-gather.6
  100.4 43.8 all-gather.4

commit v2 on v1

v2 whole, which is shorter than its diff:
```python
import functools

import jax
import jax.numpy as jnp
from jax import lax
from jax.experimental import pallas as pl
from jax.experimental.pallas import tpu as pltpu
from jax.sharding import PartitionSpec as P

HB = 1
MATS = 4
MESH = pl.DeviceIdType.MESH
F32 = jnp.float32
BF16 = jnp.bfloat16


def silu(v):
    return v / (1.0 + jnp.exp(-v))


def mm(a, b):
    return jnp.dot(a, b, preferred_element_type=F32)


def kernel(
    doms,
    samples,
    w0,
    w1,
    w2,
    w3,
    gain,
    src,
    cnt,
    tiles,
    out,
    wbuf,
    abuf,
    sbuf,
    gbuf,
    h,
    mixed,
    load_sem,
    wsend,
    wrecv,
    zrecv,
    asend,
    arecv,
    fsend,
    gsend,
    grecv,
    hsend,
    hrecv,
):
    seg = lax.axis_index("segment")
    dom = lax.axis_index("dom")
    blocks, slots, rows, _ = tiles.shape
    n = h.shape[0]
    half = n // 2
    sx = seg + 1 - 2 * lax.rem(seg, 2)
    sy = lax.rem(seg + 2, 4)
    sz = 3 - seg
    g = lax.rem(dom, 4)
    g1 = g + 1 - 2 * lax.rem(g, 2)
    g2 = lax.rem(g + 2, 4)
    g3 = 3 - g
    sib = dom + g1 - g
    zp = dom + g2 - g
    right = lax.rem(dom + 1, doms)
    left = lax.rem(dom + doms - 1, doms)

    loads = []
    for m, w in enumerate((w0, w1, w2, w3)):
        loads.append(pltpu.make_async_copy(w.at[0, 0], wbuf.at[seg, m], load_sem.at[m]))
    loads.append(pltpu.make_async_copy(samples.at[seg], h, load_sem.at[4]))
    loads.append(pltpu.make_async_copy(gain.at[0], gbuf.at[seg], load_sem.at[5]))
    for c in loads:
        c.start()

    barrier = pltpu.get_barrier_semaphore()
    for t in (sx, sy, sz):
        pl.semaphore_signal(barrier, inc=1, device_id=(t, dom), device_id_type=MESH)
    for t in (sib, zp, left, right):
        pl.semaphore_signal(barrier, inc=1, device_id=(seg, t), device_id_type=MESH)
    for c in loads:
        c.wait()
    pl.semaphore_wait(barrier, 7)

    def remote(ref, send, recv, target):
        return pltpu.make_async_remote_copy(
            src_ref=ref,
            dst_ref=ref,
            send_sem=send,
            recv_sem=recv,
            device_id=target,
            device_id_type=MESH,
        )

    tx, ty, tz, tsib, tzp = (sx, dom), (sy, dom), (sz, dom), (seg, sib), (seg, zp)

    def rows_of(which):
        return pl.ds(which * half, half)

    def w_own(i, t):
        return remote(wbuf.at[seg, g], wsend.at[i], wrecv.at[seg, g], t)

    def a_piece(i, s, part, t):
        return remote(abuf.at[s, rows_of(part)], asend.at[i], arecv.at[s, part], t)

    def g_own(i, t):
        return remote(gbuf.at[seg], gsend.at[i], grecv.at[seg], t)

    def w_relay(s, part, t):
        return remote(wbuf.at[s, g, rows_of(part)], wsend.at[2 + part], zrecv.at[part], t)

    def forward(i, s, m, t):
        return remote(wbuf.at[s, m], fsend.at[i], wrecv.at[s, m], t)

    def w_arrived(s, m):
        remote(wbuf.at[s, m], wsend.at[0], wrecv.at[s, m], tx).wait_recv()

    def a_arrived(s, part):
        a_piece(0, s, part, tx).wait_recv()

    w_own(0, tx).start()
    w_own(1, ty).start()
    for i, t in enumerate((tx, ty, tz)):
        g_own(i, t).start()

    total = blocks * doms
    first = dom * blocks
    for b in range(blocks):
        local = [lax.rem(src[0, b, k] - first + total, total) for k in range(slots)]
        count = cnt[0, b]
        vals = [tiles[b, k].astype(F32) for k in range(slots)]
        for j in range(blocks + 2 * HB):
            want = j if j <= blocks else total - 1
            acc = jnp.zeros((rows, rows), F32)
            for k in range(slots):
                hit = jnp.logical_and(local[k] == want, k < count)
                acc = acc + vals[k] * jnp.where(hit, 1.0, 0.0)
            abuf[seg, pl.ds(b * rows, rows), pl.ds(j * rows, rows)] = acc.astype(BF16)

    a_piece(0, seg, 1, tx).start()
    a_piece(1, seg, 0, ty).start()
    a_piece(2, seg, 0, tx).start()
    a_piece(3, seg, 1, ty).start()

    def adjacent_duties():
        for i, s in enumerate((sx, sy)):
            w_arrived(s, g)
            forward(3 * i, s, g, tzp).start()
            forward(3 * i + 1, s, g, tsib).start()
        w_relay(sy, 0, tx).start()
        w_relay(sx, 1, ty).start()
        for i, s in enumerate((sx, sy)):
            w_arrived(s, g2)
            forward(3 * i + 2, s, g2, tsib).start()
        a_arrived(sy, 0)
        a_piece(4, sy, 0, tx).start()
        a_arrived(sx, 1)
        a_piece(5, sx, 1, ty).start()

    def diagonal_duties():
        for part in range(2):
            w_relay(sz, part, tx).wait_recv()
        forward(6, sz, g, tzp).start()
        forward(7, sz, g, tsib).start()
        w_arrived(sz, g2)
        forward(8, sz, g2, tsib).start()

    def halo(i, s, t, lo, to):
        return pltpu.make_async_remote_copy(
            src_ref=sbuf.at[s, pl.ds(lo, rows)],
            dst_ref=sbuf.at[s, pl.ds(to, rows)],
            send_sem=hsend.at[s, i],
            recv_sem=hrecv.at[s, i],
            device_id=t,
            device_id_type=MESH,
        )

    def halos(s):
        return (
            halo(0, s, (seg, left), 0, n),
            halo(1, s, (seg, right), n - rows, n + rows),
        )

    def section(s, carry):
        @pl.when(s == jnp.where(seg == 0, 1, 0))
        def _():
            adjacent_duties()

        @pl.when(s == sz)
        def _():
            diagonal_duties()

        @pl.when(s != seg)
        def _():
            w_arrived(s, g1)
            w_arrived(s, g3)
            remote(gbuf.at[s], gsend.at[0], grecv.at[s], tx).wait_recv()

        def send_rows(lo, size):
            v = mm(h[pl.ds(lo, size), :], wbuf[s, 0])
            sbuf[s, pl.ds(lo, size), :] = silu(v).astype(BF16)

        send_rows(0, rows)
        to_left, to_right = halos(s)
        to_left.start()
        send_rows(n - rows, rows)
        to_right.start()
        send_rows(rows, n - 2 * rows)
        mixed[...] = mm(h[...], wbuf[s, 1])

        @pl.when(jnp.logical_or(s == sx, s == sz))
        def _():
            a_arrived(s, 0)

        @pl.when(jnp.logical_or(s == sy, s == sz))
        def _():
            a_arrived(s, 1)

        near = mm(abuf[s, :, pl.ds(0, n)], sbuf[s, pl.ds(0, n), :])
        to_left.wait_recv()
        to_right.wait_recv()
        far = mm(abuf[s, :, pl.ds(n, 2 * rows)], sbuf[s, pl.ds(n, 2 * rows), :])
        gathered = (near + far).astype(BF16)
        mix = mixed[...] + mm(gathered, wbuf[s, 2])
        scale = lax.rsqrt(jnp.mean(mix * mix, axis=-1, keepdims=True) + 1e-05)
        update = silu(mix * scale * gbuf[s]).astype(BF16)
        h[...] = (h[...].astype(F32) + mm(update, wbuf[s, 3])).astype(BF16)
        return carry

    lax.fori_loop(0, 4, section, 0)
    out[...] = h[...]

    w_own(0, tx).wait_send()
    w_own(1, ty).wait_send()
    for i, t in enumerate((tx, ty, tz)):
        g_own(i, t).wait_send()
    for part in range(2):
        w_relay(sx, part, tx).wait_send()
    for i in range(6):
        a_piece(i, seg, 0, tx).wait_send()
    for i in range(9):
        forward(i, sx, g, tsib).wait_send()
    for s in range(4):
        for c in halos(s):
            c.wait_send()


def shards(
    samples, w_source, w_self, w_message, w_output, norm_gain, tile_source, tile_count, tile_value
):
    sections = lax.axis_size("segment")
    doms = lax.axis_size("dom")
    assert sections == 4 and samples.shape[0] == 4 and doms % 4 == 0
    _, n, width = samples.shape
    _, blocks, slots, rows, _ = tile_value.shape
    window = (blocks + 2 * HB) * rows
    dma = pltpu.SemaphoreType.DMA
    any_space = pl.BlockSpec(memory_space=pl.ANY)
    smem = pl.BlockSpec(memory_space=pltpu.SMEM)
    vmem = pl.BlockSpec(memory_space=pltpu.VMEM)
    out = pl.pallas_call(
        functools.partial(kernel, doms),
        out_shape=jax.ShapeDtypeStruct((n, width), BF16),
        in_specs=[any_space] * 6 + [smem, smem, vmem],
        out_specs=vmem,
        scratch_shapes=[
            pltpu.VMEM((sections, MATS, width, width), BF16),
            pltpu.VMEM((sections, n, window), BF16),
            pltpu.VMEM((sections, window, width), BF16),
            pltpu.VMEM((sections, 1, width), F32),
            pltpu.VMEM((n, width), BF16),
            pltpu.VMEM((n, width), F32),
            dma((6,)),
            dma((4,)),
            dma((sections, MATS)),
            dma((2,)),
            dma((6,)),
            dma((sections, 2)),
            dma((9,)),
            dma((3,)),
            dma((sections,)),
            dma((sections, 2)),
            dma((sections, 2)),
        ],
        compiler_params=pltpu.CompilerParams(
            collective_id=0, has_side_effects=True, vmem_limit_bytes=56 * 1024 * 1024
        ),
    )(
        samples,
        w_source,
        w_self,
        w_message,
        w_output,
        norm_gain,
        tile_source,
        tile_count,
        tile_value[0],
    )
    return out[None]


def solution(mesh):
    return jax.shard_map(
        shards,
        mesh=mesh,
        in_specs=(
            P(None, "dom", None),
            P("segment", None, None, None),
            P("segment", None, None, None),
            P("segment", None, None, None),
            P("segment", None, None, None),
            P("segment", None, None),
            P("segment", "dom", None),
            P("segment", "dom"),
            P("segment", "dom", None, None, None),
        ),
        out_specs=P("segment", "dom", None),
        check_vma=False,
    )
```

time: 200 us -> 84.6 us (0.42); the launches traced: 197 us -> 84.3 us
  waiting for transfers between devices: 121 us -> 0 us
  Pallas kernels: 0 us -> 82.5 us
  matrix products: 32.9 us -> 0 us
  starting transfers between devices: 13.7 us -> 0 us
  between operations: 13.7 us -> 0.01 us
  blocking collectives: 8.07 us -> 0 us
  other arithmetic: 4.53 us -> 0 us
    all_gather x2 -> x0, waiting for transfers between devices: 116 us -> none  [the longest x1 76.9 us: shards(): weights = lax.all_gather(weights, 'segment')]
    pallas_call x0 -> x1, Pallas kernels: none -> 82.5 us  [shards(): pl.pallas_call(functools.partial(kernel, doms), out_shape=jax.ShapeDtypeS...]
    dot_general x16 -> x0, matrix products: 32.9 us -> none  [the longest x4 11.3 us: shards(): jnp.dot(gathered, wc, preferred_element_type=jnp.float32)]
    ppermute x8 -> x0, starting transfers between devices: 13.7 us -> none  [the longest x4 12.3 us: from_neighbours(): lax.ppermute(head, 'dom', [((i + 1) % count, i) for i in range(count)])]
    all_gather x1 -> x0, blocking collectives: 8.07 us -> none  [shards(): gains = lax.all_gather(norm_gain[0, 0], 'segment')]
    ppermute x8 -> x0, waiting for transfers between devices: 5.56 us -> none  [the longest x4 5.55 us: from_neighbours(): lax.ppermute(tail, 'dom', [(i, (i + 1) % count) for i in range(count)])]
    concatenate x1 -> x0, other arithmetic: 3.18 us -> none  [shards(): jnp.concatenate([w_source[0, 0], w_self[0, 0], w_message[0, 0], w_output[...]
    convert_element_type x2 -> x0, local copies, waits for them, and re-layouts: 2.33 us -> none  [dense_edges(): return dense.reshape(blocks * rows, window * rows).astype(jnp.bfloat16)]
  transfers between devices with their start and end apart: 10 -> 0, of which waited for: 5 -> 0; matrix products, arithmetic and copies ran while one was open for 6% -> 0% of each run, Pallas kernels for 0% -> 0%
where the time goes in v2:
time: 84.6 us; the launch traced here: 84.3 us
  Pallas kernels  82.5 us (98%)
  local copies, waits for them, and re-layouts  1.87 us (2%)
    pallas_call x1, Pallas kernels, shards(): pl.pallas_call(functools.partial(kernel, doms), out_shape=jax.ShapeDtypeS...  82.5 us
    unnamed x1, local copies, waits for them, and re-layouts  1.87 us

profile of v2, /device:TPU:4, one launch (start us, length us, event | category | flops | bytes accessed | tf_op | source)
XLA Modules:
  0.0 84.3 jit_solution(15960485785343040800)
XLA Ops:
  0.0 82.5 %shard_map.91 = bf16[512,512]{1,0:T(8,128)(2,1)} custom-call(bf16[4,512,512]{2,1,0:T(8,128)(2,1)} %samples.1, bf16[1,1,512,512]{3,2,1,0:T(8,128)(2,1)} %w0.1, bf16[1,1,512,512]{3,2,1,0:T(8,128)(2,1)} %w1.1, bf16[1,1,512,512]{3,2,1,0:T(8,128)(2,1)} %w2.1, bf16[1,1,512,512]{3,2,1,0:T(8,128)(2,1)} %w3.1, f32[1,1,512]{2,1,0:T(1,128)} %gain.1, s32[1,4,6]{2,1,0:T(4,128)} %src.1, ...), custom_call_target="tpu_custom_call" | custom-call | tf_op jit(solution)/shard_map/pallas_call | solution.py:265
  82.5 1.9 %copy.11 = bf16[1,512,512]{2,1,0:T(8,128)(2,1)} copy(bf16[1,512,512]{2,1,0:T(8,128)(2,1)} %bitcast.2) | data formatting | bytes 1048576

commit v3 on v2

--- a/solution.py
+++ b/solution.py
@@ -141,33 +141,79 @@
                 acc = acc + vals[k] * jnp.where(hit, 1.0, 0.0)
             abuf[seg, pl.ds(b * rows, rows), pl.ds(j * rows, rows)] = acc.astype(BF16)
 
-    a_piece(0, seg, 1, tx).start()
-    a_piece(1, seg, 0, ty).start()
-    a_piece(2, seg, 0, tx).start()
-    a_piece(3, seg, 1, ty).start()
-
-    def adjacent_duties():
-        for i, s in enumerate((sx, sy)):
-            w_arrived(s, g)
-            forward(3 * i, s, g, tzp).start()
-            forward(3 * i + 1, s, g, tsib).start()
+    hold_x = sy < seg
+    hold_y = sx < seg
+
+    def own_x(first, second):
+        if first:
+            a_piece(0, seg, 1, tx).start()
+        if second:
+            a_piece(2, seg, 0, tx).start()
+
+    def own_y(first, second):
+        if first:
+            a_piece(1, seg, 0, ty).start()
+        if second:
+            a_piece(3, seg, 1, ty).start()
+
+    @pl.when(seg == 0)
+    def _():
+        own_x(True, False)
+        own_y(True, False)
+
+    lowest = jnp.where(seg == 0, 1, 0)
+
+    def weight_duties():
+        w_arrived(sx, g)
+        w_arrived(sy, g)
         w_relay(sy, 0, tx).start()
         w_relay(sx, 1, ty).start()
-        for i, s in enumerate((sx, sy)):
-            w_arrived(s, g2)
-            forward(3 * i + 2, s, g2, tsib).start()
+
+        @pl.when(seg == 0)
+        def _():
+            own_x(False, True)
+            own_y(False, True)
+
+        @pl.when(jnp.logical_and(seg != 0, jnp.logical_not(hold_x)))
+        def _():
+            own_x(True, True)
+
+        @pl.when(jnp.logical_and(seg != 0, jnp.logical_not(hold_y)))
+        def _():
+            own_y(True, True)
+
+        for k in range(3):
+            s = k + jnp.where(seg <= k, 1, 0)
+
+            @pl.when(s == sz)
+            def _():
+                for part in range(2):
+                    w_relay(sz, part, tx).wait_recv()
+
+            forward(3 * k, s, g, tzp).start()
+            forward(3 * k + 1, s, g, tsib).start()
+        w_arrived(lowest, g2)
+        forward(2, lowest, g2, tsib).start()
+
+    def relay_from_y():
         a_arrived(sy, 0)
         a_piece(4, sy, 0, tx).start()
+
+        @pl.when(hold_x)
+        def _():
+            own_x(True, True)
+
+    def relay_from_x():
         a_arrived(sx, 1)
         a_piece(5, sx, 1, ty).start()
 
-    def diagonal_duties():
-        for part in range(2):
-            w_relay(sz, part, tx).wait_recv()
-        forward(6, sz, g, tzp).start()
-        forward(7, sz, g, tsib).start()
-        w_arrived(sz, g2)
-        forward(8, sz, g2, tsib).start()
+        @pl.when(hold_y)
+        def _():
+            own_y(True, True)
+
+    ends = jnp.logical_or(seg == 0, seg == 3)
+    from_x_at = jnp.where(ends, 1, jnp.where(seg == 1, 0, 2))
+    from_y_at = jnp.where(ends, 1, jnp.where(seg == 1, 2, 0))
 
     def halo(i, s, t, lo, to):
         return pltpu.make_async_remote_copy(
@@ -186,13 +232,17 @@
         )
 
     def section(s, carry):
-        @pl.when(s == jnp.where(seg == 0, 1, 0))
-        def _():
-            adjacent_duties()
-
-        @pl.when(s == sz)
-        def _():
-            diagonal_duties()
+        @pl.when(s == lowest)
+        def _():
+            weight_duties()
+
+        @pl.when(s == from_y_at)
+        def _():
+            relay_from_y()
+
+        @pl.when(s == from_x_at)
+        def _():
+            relay_from_x()
 
         @pl.when(s != seg)
         def _():
@@ -221,6 +271,14 @@
             a_arrived(s, 1)
 
         near = mm(abuf[s, :, pl.ds(0, n)], sbuf[s, pl.ds(0, n), :])
+
+        later = s + 1
+
+        @pl.when(jnp.logical_and(later < 4, jnp.logical_and(later != seg, later != lowest)))
+        def _():
+            w_arrived(later, g2)
+            forward(jnp.where(later - jnp.where(later > seg, 1, 0) == 1, 5, 8), later, g2, tsib).start()
+
         to_left.wait_recv()
         to_right.wait_recv()
         far = mm(abuf[s, :, pl.ds(n, 2 * rows)], sbuf[s, pl.ds(n, 2 * rows), :])

time: 84.6 us -> 97 us (1.15); the launches traced: 84.3 us -> 95.6 us
  Pallas kernels: 82.5 us -> 93.7 us
    pallas_call x1, Pallas kernels: 82.5 us -> 93.7 us  [shards(): pl.pallas_call(functools.partial(kernel, doms), out_shape=jax.ShapeDtypeS...]
where the time goes in v3:
time: 97 us; the launch traced here: 95.6 us
  Pallas kernels  93.7 us (97%)
  local copies, waits for them, and re-layouts  1.87 us (2%)
    pallas_call x1, Pallas kernels, shards(): pl.pallas_call(functools.partial(kernel, doms), out_shape=jax.ShapeDtypeS...  93.7 us

profile of v3, /device:TPU:4, one launch (start us, length us, event | category | flops | bytes accessed | tf_op | source)
XLA Modules:
  0.0 95.6 jit_solution(14530805247216699319)
XLA Ops:
  0.0 93.7 %shard_map.91 = bf16[512,512]{1,0:T(8,128)(2,1)} custom-call(bf16[4,512,512]{2,1,0:T(8,128)(2,1)} %samples.1, bf16[1,1,512,512]{3,2,1,0:T(8,128)(2,1)} %w0.1, bf16[1,1,512,512]{3,2,1,0:T(8,128)(2,1)} %w1.1, bf16[1,1,512,512]{3,2,1,0:T(8,128)(2,1)} %w2.1, bf16[1,1,512,512]{3,2,1,0:T(8,128)(2,1)} %w3.1, f32[1,1,512]{2,1,0:T(1,128)} %gain.1, s32[1,4,6]{2,1,0:T(4,128)} %src.1, ...), custom_call_target="tpu_custom_call" | custom-call | tf_op jit(solution)/shard_map/pallas_call | solution.py:323
  93.7 1.9 %copy.11 = bf16[1,512,512]{2,1,0:T(8,128)(2,1)} copy(bf16[1,512,512]{2,1,0:T(8,128)(2,1)} %bitcast.2) | data formatting | bytes 1048576

commit v4 on v2

--- a/solution.py
+++ b/solution.py
@@ -166,6 +166,8 @@
             w_relay(sz, part, tx).wait_recv()
         forward(6, sz, g, tzp).start()
         forward(7, sz, g, tsib).start()
+
+    def diagonal_last():
         w_arrived(sz, g2)
         forward(8, sz, g2, tsib).start()
 
@@ -189,10 +191,11 @@
         @pl.when(s == jnp.where(seg == 0, 1, 0))
         def _():
             adjacent_duties()
+            diagonal_duties()
 
         @pl.when(s == sz)
         def _():
-            diagonal_duties()
+            diagonal_last()
 
         @pl.when(s != seg)
         def _():
@@ -232,7 +235,8 @@
         return carry
 
     lax.fori_loop(0, 4, section, 0)
-    out[...] = h[...]
+    final = pltpu.make_async_copy(h, out.at[0], load_sem.at[0])
+    final.start()
 
     w_own(0, tx).wait_send()
     w_own(1, ty).wait_send()
@@ -247,6 +251,7 @@
     for s in range(4):
         for c in halos(s):
             c.wait_send()
+    final.wait()
 
 
 def shards(
@@ -264,9 +269,9 @@
     vmem = pl.BlockSpec(memory_space=pltpu.VMEM)
     out = pl.pallas_call(
         functools.partial(kernel, doms),
-        out_shape=jax.ShapeDtypeStruct((n, width), BF16),
+        out_shape=jax.ShapeDtypeStruct((1, n, width), BF16),
         in_specs=[any_space] * 6 + [smem, smem, vmem],
-        out_specs=vmem,
+        out_specs=any_space,
         scratch_shapes=[
             pltpu.VMEM((sections, MATS, width, width), BF16),
             pltpu.VMEM((sections, n, window), BF16),
@@ -300,7 +305,7 @@
         tile_count,
         tile_value[0],
     )
-    return out[None]
+    return out
 
 
 def solution(mesh):

time: 84.6 us -> 81.1 us (0.959)
  the two profiles are of different devices: /device:TPU:4 before, /device:TPU:7 now
where the time goes in v4:
time: 81.1 us; the launch traced here: 80.9 us
  Pallas kernels  79 us (97%)
  local copies, waits for them, and re-layouts  1.87 us (2%)
    pallas_call x1, Pallas kernels, shards(): pl.pallas_call(functools.partial(kernel, doms), out_shape=jax.ShapeDtypeS...  79 us
    unnamed x1, local copies, waits for them, and re-layouts  1.87 us

profile of v4, /device:TPU:7, one launch (start us, length us, event | category | flops | bytes accessed | tf_op | source)
XLA Modules:
  0.0 80.9 jit_solution(10454938871595862873)
XLA Ops:
  0.0 79.0 %shard_map.91 = bf16[1,512,512]{2,1,0:T(8,128)(2,1)} custom-call(bf16[4,512,512]{2,1,0:T(8,128)(2,1)} %samples.1, bf16[1,1,512,512]{3,2,1,0:T(8,128)(2,1)} %w0.1, bf16[1,1,512,512]{3,2,1,0:T(8,128)(2,1)} %w1.1, bf16[1,1,512,512]{3,2,1,0:T(8,128)(2,1)} %w2.1, bf16[1,1,512,512]{3,2,1,0:T(8,128)(2,1)} %w3.1, f32[1,1,512]{2,1,0:T(1,128)} %gain.1, ...), custom_call_target="tpu_custom_call" | custom-call | tf_op jit(solution)/shard_map/pallas_call | solution.py:270
  79.0 1.9 %copy.11 = bf16[1,512,512]{2,1,0:T(8,128)(2,1)} copy(bf16[1,512,512]{2,1,0:T(8,128)(2,1)} %shard_map.91) | data formatting | bytes 1048576
